TPU v7x, 128 devices: a whole 4x4x4 slice. The times are simulated.
128 devices in a mesh: row: 8 (over x_lo, z), col: 16 (over x_hi, y, core).
Axes of the slice: x: 4 (x_hi: 2, x_lo: 2; x = x_hi * 2 + x_lo), y: 4, z: 4, core: 2. Of those that a mesh axis runs over, the one named last changes fastest.
Arguments:
- hessian: float32 [18432, 18432], P('row', 'col'), may hold values from -1 to 5, as said below
- right_side: float32 [18432, 512], P('row'), may hold values from -6 to 6
- mask: int32 [18432, 512], P('row'), may hold values 0 or 1
- damping: float32 [1], replicated, may hold values from 0.4 to 1.2
Outputs:
- solution: float32 [18432, 512], P('row')
Inputs may be any that keep to these rules, and one draw needn't show every extreme that they name: hessian is symmetric and positive definite.
All inputs are finite; a program needn't handle non-finite values. No bound on the sum of `mask` on one device may be relied on, other than what follows from the above.
Results may differ from a plain program's by a relative error of at most 0.0001.
Values sent between devices are 32-bit elements; how exact they have to be, the bound alone decides.
A program may use at most 128 MiB of HBM per device.

v0:
```python
import jax
import jax.numpy as jnp
from jax import lax
from jax.sharding import PartitionSpec as P

ITERS = 3
epsilon = 1e-06


def in_one(arrays, axis):
    ends = [0]
    for a in arrays:
        ends.append(ends[-1] + a.size)
    so_far = lax.psum(jnp.concatenate([a.ravel() for a in arrays]), axis)
    return tuple((so_far[b:e].reshape(a.shape) for a, b, e in zip(arrays, ends, ends[1:])))


def from_root(block, axis, source):
    block = jnp.where(lax.axis_index(axis) == source, block, jnp.zeros_like(block))
    return lax.psum(block, axis)


def rows_for(lines, peers):
    spare = -len(lines) % peers
    return jnp.pad(lines, [(0, spare)] + [(0, 0)] * (lines.ndim - 1))


def sum_by_parts(array, axis):
    lines = array.reshape(-1, *array.shape[1:][-1:])
    own = lax.psum_scatter(
        rows_for(lines, lax.axis_size(axis)), axis, scatter_dimension=0, tiled=True
    )
    whole = lax.all_gather(own, axis).reshape(-1, *lines.shape[1:])
    return lax.slice_in_dim(whole, 0, len(lines)).reshape(array.shape)


def column_sums(first, second):
    return jnp.sum(first * second, axis=0)


def both_sums(residual, applied):
    return in_one((column_sums(residual, residual), column_sums(residual, applied)), "row")


def on_device(hessian, right_side, mask, damping):
    mask_float = mask.astype(jnp.float32)
    damping_value = damping[0]
    blocks_ratio = lax.axis_size("col") // lax.axis_size("row")
    block_width = hessian.shape[1]
    col_position = lax.axis_index("col")

    def masked_apply(vector):
        own_slice = lax.dynamic_slice_in_dim(
            vector, col_position % blocks_ratio * block_width, block_width, 0
        )
        column_block = from_root(own_slice, "row", col_position // blocks_ratio)
        partial_value = jnp.dot(
            hessian,
            column_block,
            precision=lax.Precision.HIGHEST,
            preferred_element_type=jnp.float32,
        )
        summed = sum_by_parts(partial_value, "col")
        return mask_float * (summed + damping_value * vector)

    residual = mask_float * right_side
    direction = residual
    solution = jnp.zeros_like(right_side)
    applied = masked_apply(residual)
    norm_now, inner = both_sums(residual, applied)
    step_size = norm_now / (inner + epsilon)
    along = applied
    for iteration in range(ITERS):
        solution = solution + step_size * direction
        residual = residual - step_size * along
        if iteration + 1 < ITERS:
            applied = masked_apply(residual)
            norm_next, inner = both_sums(residual, applied)
            factor = norm_next / (norm_now + epsilon)
            curvature = inner - factor * norm_next / step_size
            step_size = norm_next / (curvature + epsilon)
            direction = residual + factor * direction
            along = applied + factor * along
            norm_now = norm_next
    return solution


def solution(mesh):
    in_specs = (P("row", "col"), P("row", None), P("row", None), P())
    out_specs = P("row", None)
    return jax.shard_map(
        on_device, mesh=mesh, in_specs=in_specs, out_specs=out_specs, check_vma=False
    )
```

profile of v0, /device:TPU:0, one launch (start us, length us, event | category | flops | bytes accessed | tf_op | source)
XLA Modules:
  0.0 936.5 jit_solution(12849361006295928117)
XLA Ops:
  6.5 0.0 all-reduce.4.cloned.1.call-start
  6.5 4.9 convert_multiply_fusion
  11.5 0.0 copy-start
  11.5 2.2 copy-done
  13.7 1.7 dynamic-slice_select_fusion.2
  15.3 0.0 all-reduce.4.cloned.1.call-update
  15.4 0.0 reduce-scatter.10.cloned.1.call-start
  15.4 86.8 %all-reduce.4.cloned.1.call-done = f32[1152,512]{1,0:T(8,128)} async-done(((f32[1152,512]{1,0:T(8,128)}), f32[1152,512]{1,0:T(8,128)}) %all-reduce.4.cloned.1.call-update) | async-done | bytes 2359312 | tf_op jit(solution)/shard_map/psum | solution.py:20
  102.2 37.5 %convolution_bitcast_fusion.2 = f32[2304,512]{0,1:T(8,128)} fusion(f32[1152,512]{1,0:T(8,128)} %all-reduce.4.cloned.1.call-done, f32[2304,1152]{1,0:T(8,128)} %param.4), kind=kOutput, calls=%fused_computation.2 | convolution fusion | flops 16307453952 | bytes 17694720 | tf_op jit(solution)/shard_map/dot_general | solution.py:57
  139.7 6.1 copy.11
  145.8 0.0 reduce-scatter.10.cloned.1.call-update
  145.9 0.0 all-gather.7.cloned.1.call-start
  145.9 82.9 %reduce-scatter.10.cloned.1.call-done = f32[144,512]{1,0:T(8,128)} async-done(((f32[2304,512]{1,0:T(8,128)}), f32[144,512]{1,0:T(8,128)}) %reduce-scatter.10.cloned.1.call-update) | async-done | bytes 294928 | tf_op jit(solution)/shard_map/reduce_scatter | solution.py:30
  228.8 0.0 all-gather.7.cloned.1.call-update
  228.9 0.2 all-reduce.6.cloned.1.call-start
  229.7 58.0 %all-gather.7.cloned.1.call-done = f32[2304,512]{1,0:T(8,128)} async-done(((f32[144,512]{1,0:T(8,128)}), f32[2304,512]{1,0:T(8,128)}) %all-gather.7.cloned.1.call-update) | async-done | bytes 4718608 | tf_op jit(solution)/shard_map/all_gather | solution.py:33
  287.8 6.9 multiply_reduce_fusion.5
  294.7 18.9 %psum.43 = f32[1024]{0:T(1024)S(1)} all-reduce(f32[1024]{0:T(1024)S(1)} %pad_maximum_fusion), channel_id=1, replica_groups=mesh['row'=8,'col'=16] {'row'}, use_global_device_ids=true, to_apply=%region_4.5 | all-reduce | flops 1024 | bytes 8192 | tf_op jit(solution)/shard_map/psum | solution.py:14
  313.6 6.9 multiply_subtract_fusion.1
  320.5 0.0 copy-start.1
  320.6 2.1 copy-done.1
  322.7 1.7 dynamic-slice_select_fusion.1
  324.3 0.0 all-reduce.6.cloned.1.call-update
  324.4 0.0 reduce-scatter.12.cloned.1.call-start
  324.4 80.6 %all-reduce.6.cloned.1.call-done = f32[1152,512]{1,0:T(8,128)} async-done(((f32[1152,512]{1,0:T(8,128)}), f32[1152,512]{1,0:T(8,128)}) %all-reduce.6.cloned.1.call-update) | async-done | bytes 2359312 | tf_op jit(solution)/shard_map/psum | solution.py:20
  405.0 37.5 %convolution_bitcast_fusion.1 = f32[2304,512]{0,1:T(8,128)} fusion(f32[1152,512]{1,0:T(8,128)} %all-reduce.6.cloned.1.call-done, f32[2304,1152]{1,0:T(8,128)} %param.4), kind=kOutput, calls=%fused_computation.1 | convolution fusion | flops 16307453952 | bytes 17694720 | tf_op jit(solution)/shard_map/dot_general | solution.py:57
  442.5 6.1 copy.13
  448.5 0.0 reduce-scatter.12.cloned.1.call-update
  448.6 0.0 all-gather.9.cloned.1.call-start
  448.6 83.0 %reduce-scatter.12.cloned.1.call-done = f32[144,512]{1,0:T(8,128)} async-done(((f32[2304,512]{1,0:T(8,128)}), f32[144,512]{1,0:T(8,128)}) %reduce-scatter.12.cloned.1.call-update) | async-done | bytes 294928 | tf_op jit(solution)/shard_map/reduce_scatter | solution.py:30
  531.6 0.0 all-gather.9.cloned.1.call-update
  531.6 0.3 all-reduce.8.cloned.1.call-start
  531.9 58.1 %all-gather.9.cloned.1.call-done = f32[2304,512]{1,0:T(8,128)} async-done(((f32[144,512]{1,0:T(8,128)}), f32[2304,512]{1,0:T(8,128)}) %all-gather.9.cloned.1.call-update) | async-done | bytes 4718608 | tf_op jit(solution)/shard_map/all_gather | solution.py:33
  590.0 6.9 multiply_reduce_fusion.3
  596.9 18.9 %psum.45 = f32[1024]{0:T(1024)S(1)} all-reduce(f32[1024]{0:T(1024)S(1)} %pad_maximum_fusion.1), channel_id=1, replica_groups=mesh['row'=8,'col'=16] {'row'}, use_global_device_ids=true, to_apply=%region_9.10 | all-reduce | flops 1024 | bytes 8192 | tf_op jit(solution)/shard_map/psum | solution.py:14
  615.9 8.7 multiply_subtract_fusion
  624.5 0.0 copy-start.2
  624.6 2.2 copy-done.2
  626.7 1.7 dynamic-slice_select_fusion
  628.4 0.0 all-reduce.8.cloned.1.call-update
  628.4 0.0 reduce-scatter.14.cloned.1.call-start
  628.4 80.6 %all-reduce.8.cloned.1.call-done = f32[1152,512]{1,0:T(8,128)} async-done(((f32[1152,512]{1,0:T(8,128)}), f32[1152,512]{1,0:T(8,128)}) %all-reduce.8.cloned.1.call-update) | async-done | bytes 2359312 | tf_op jit(solution)/shard_map/psum | solution.py:20
  709.0 37.5 %convolution_bitcast_fusion = f32[2304,512]{0,1:T(8,128)} fusion(f32[1152,512]{1,0:T(8,128)} %all-reduce.8.cloned.1.call-done, f32[2304,1152]{1,0:T(8,128)} %param.4), kind=kOutput, calls=%fused_computation | convolution fusion | flops 16307453952 | bytes 17694720 | tf_op jit(solution)/shard_map/dot_general | solution.py:57
  746.5 6.1 copy.15
  752.6 0.0 reduce-scatter.14.cloned.1.call-update
  752.6 0.3 all-gather.11.cloned.1.call-start
  752.9 82.7 %reduce-scatter.14.cloned.1.call-done = f32[144,512]{1,0:T(8,128)} async-done(((f32[2304,512]{1,0:T(8,128)}), f32[144,512]{1,0:T(8,128)}) %reduce-scatter.14.cloned.1.call-update) | async-done | bytes 294928 | tf_op jit(solution)/shard_map/reduce_scatter | solution.py:30
  835.6 0.0 all-gather.11.cloned.1.call-update
  835.6 58.9 %all-gather.11.cloned.1.call-done = f32[2304,512]{1,0:T(8,128)} async-done(((f32[144,512]{1,0:T(8,128)}), f32[2304,512]{1,0:T(8,128)}) %all-gather.11.cloned.1.call-update) | async-done | bytes 4718608 | tf_op jit(solution)/shard_map/all_gather | solution.py:33
  894.5 6.9 multiply_reduce_fusion.1
  901.5 18.9 %psum.47 = f32[1024]{0:T(1024)S(1)} all-reduce(f32[1024]{0:T(1024)S(1)} %pad_maximum_fusion.2), channel_id=1, replica_groups=mesh['row'=8,'col'=16] {'row'}, use_global_device_ids=true, to_apply=%region_14.15 | all-reduce | flops 1024 | bytes 8192 | tf_op jit(solution)/shard_map/psum | solution.py:14
  920.4 9.2 multiply_add_fusion
  (6 shorter events, 0.1 us)
Async XLA Ops:
  6.5 95.7 %all-reduce.4.cloned.1.call-start = ((), (), s32[]{:S(2)}) async-start(), calls=%async_computation.3 | async-start | bytes 4718592 | tf_op jit(solution)/shard_map/psum | solution.py:20
  11.5 2.2 copy-start
  15.4 213.5 %reduce-scatter.10.cloned.1.call-start = ((), (), s32[]{:S(2)}) async-start(), calls=%async_computation.9 | async-start | bytes 5013504 | tf_op jit(solution)/shard_map/reduce_scatter | solution.py:30
  145.9 141.9 %all-gather.7.cloned.1.call-start = ((), (), s32[]{:S(2)}) async-start(), calls=%async_computation.6 | async-start | bytes 5013504 | tf_op jit(solution)/shard_map/all_gather | solution.py:33
  228.9 176.1 %all-reduce.6.cloned.1.call-start = ((), (), s32[]{:S(2)}) async-start(), calls=%async_computation.4 | async-start | bytes 4718592 | tf_op jit(solution)/shard_map/psum | solution.py:20
  320.5 2.1 copy-start.1
  324.4 207.2 %reduce-scatter.12.cloned.1.call-start = ((), (), s32[]{:S(2)}) async-start(), calls=%async_computation.10 | async-start | bytes 5013504 | tf_op jit(solution)/shard_map/reduce_scatter | solution.py:30
  448.6 141.4 %all-gather.9.cloned.1.call-start = ((), (), s32[]{:S(2)}) async-start(), calls=%async_computation.7 | async-start | bytes 5013504 | tf_op jit(solution)/shard_map/all_gather | solution.py:33
  531.6 177.4 %all-reduce.8.cloned.1.call-start = ((), (), s32[]{:S(2)}) async-start(), calls=%async_computation.5 | async-start | bytes 4718592 | tf_op jit(solution)/shard_map/psum | solution.py:20
  624.5 2.2 copy-start.2
  628.4 207.2 %reduce-scatter.14.cloned.1.call-start = ((), (), s32[]{:S(2)}) async-start(), calls=%async_computation.11 | async-start | bytes 5013504 | tf_op jit(solution)/shard_map/reduce_scatter | solution.py:30
  752.6 141.9 %all-gather.11.cloned.1.call-start = ((), (), s32[]{:S(2)}) async-start(), calls=%async_computation.8 | async-start | bytes 5013504 | tf_op jit(solution)/shard_map/all_gather | solution.py:33
Sparse Core Ops, SparseCore 0:
  15.5 86.6 all-reduce.3
  146.0 82.7 reduce-scatter.9
  231.6 56.1 all-gather.6
  324.5 80.4 all-reduce.5
  448.7 82.8 reduce-scatter.11
  533.9 56.0 all-gather.8
  628.5 80.4 all-reduce.7
  752.7 82.8 reduce-scatter.13
  838.4 56.0 all-gather.10
where the time goes:
time: 946 us; the launch traced here: 937 us
  waiting for transfers between devices  672 us (71%)
  matrix products  112 us (12%)
  blocking collectives  56.7 us (6%)
  other arithmetic  55.5 us (6%)
  local copies, waits for them, and re-layouts  24.8 us (3%)
  between operations  14.3 us (2%)
    reduce_scatter x3, waiting for transfers between devices, sum_by_parts(): lax.psum_scatter(rows_for(lines, lax.axis_size(axis)), axis, scatter_dime...  249 us
    psum x3, waiting for transfers between devices, from_root(): return lax.psum(block, axis)  248 us
    all_gather x3, waiting for transfers between devices, sum_by_parts(): whole = lax.all_gather(own, axis).reshape(-1, *lines.shape[1:])  175 us
    dot_general x3, matrix products, masked_apply(): jnp.dot(hessian, column_block, precision=lax.Precision.HIGHEST, preferred...  112 us
    psum x3, blocking collectives, in_one(): so_far = lax.psum(jnp.concatenate([a.ravel() for a in arrays]), axis)  56.7 us
    unnamed x9, local copies, waits for them, and re-layouts  24.8 us
    reduce_sum x3, other arithmetic, column_sums(): return jnp.sum(first * second, axis=0)  20.8 us
  transfers between devices with their start and end apart: 9, of which 9 were waited for; matrix products, arithmetic and copies ran while one was open for 0% of the time, Pallas kernels for 0%

commit v1 on v0

--- a/solution.py
+++ b/solution.py
@@ -11,7 +11,7 @@
     ends = [0]
     for a in arrays:
         ends.append(ends[-1] + a.size)
-    so_far = lax.psum(jnp.concatenate([a.ravel() for a in arrays]), axis)
+    so_far = jnp.sum(lax.all_gather(jnp.concatenate([a.ravel() for a in arrays]), axis), axis=0)
     return tuple((so_far[b:e].reshape(a.shape) for a, b, e in zip(arrays, ends, ends[1:])))
 
 

time: 946 us -> 977 us (1.033)
  blocking collectives: 56.7 us -> 84.2 us
    all_gather x0 -> x3, blocking collectives: none -> 84.2 us  [in_one(): lax.all_gather(jnp.concatenate([a.ravel() for a in arrays]), axis)]
    psum x3 -> x0, blocking collectives: 56.7 us -> none  [in_one(): so_far = lax.psum(jnp.concatenate([a.ravel() for a in arrays]), axis)]
where the time goes in v1:
time: 977 us; the launch traced here: 967 us
  waiting for transfers between devices  675 us (69%)
  matrix products  112 us (11%)
  blocking collectives  84.2 us (9%)
  other arithmetic  55.6 us (6%)
  local copies, waits for them, and re-layouts  24.8 us (3%)
  between operations  14.4 us (1%)
    psum x3, waiting for transfers between devices, from_root(): return lax.psum(block, axis)  251 us
    reduce_scatter x3, waiting for transfers between devices, sum_by_parts(): lax.psum_scatter(rows_for(lines, lax.axis_size(axis)), axis, scatter_dime...  249 us
    all_gather x3, waiting for transfers between devices, sum_by_parts(): whole = lax.all_gather(own, axis).reshape(-1, *lines.shape[1:])  175 us
    dot_general x3, matrix products, masked_apply(): jnp.dot(hessian, column_block, precision=lax.Precision.HIGHEST, preferred...  112 us
    all_gather x3, blocking collectives, in_one(): lax.all_gather(jnp.concatenate([a.ravel() for a in arrays]), axis)  84.2 us
    unnamed x9, local copies, waits for them, and re-layouts  24.8 us
    reduce_sum x3, other arithmetic, column_sums(): return jnp.sum(first * second, axis=0)  20.8 us
  transfers between devices with their start and end apart: 9, of which 9 were waited for; matrix products, arithmetic and copies ran while one was open for 0% of the time, Pallas kernels for 0%

profile of v1, /device:TPU:0, one launch (start us, length us, event | category | flops | bytes accessed | tf_op | source)
XLA Modules:
  0.0 967.0 jit_solution(11126204946080373285)
XLA Ops:
  6.5 0.0 all-reduce.4.cloned.1.call-start
  6.5 4.9 convert_multiply_fusion
  11.5 0.0 copy-start
  11.5 2.2 copy-done
  13.7 1.7 dynamic-slice_select_fusion.2
  15.3 0.0 all-reduce.4.cloned.1.call-update
  15.4 0.0 reduce-scatter.10.cloned.1.call-start
  15.4 86.8 %all-reduce.4.cloned.1.call-done = f32[1152,512]{1,0:T(8,128)} async-done(((f32[1152,512]{1,0:T(8,128)}), f32[1152,512]{1,0:T(8,128)}) %all-reduce.4.cloned.1.call-update) | async-done | bytes 2359312 | tf_op jit(solution)/shard_map/psum | solution.py:20
  102.2 37.5 %convolution_bitcast_fusion.2 = f32[2304,512]{0,1:T(8,128)} fusion(f32[1152,512]{1,0:T(8,128)} %all-reduce.4.cloned.1.call-done, f32[2304,1152]{1,0:T(8,128)} %param.4), kind=kOutput, calls=%fused_computation.2 | convolution fusion | flops 16307453952 | bytes 17694720 | tf_op jit(solution)/shard_map/dot_general | solution.py:57
  139.7 6.1 copy.14
  145.8 0.0 reduce-scatter.10.cloned.1.call-update
  145.9 0.0 all-gather.10.cloned.1.call-start
  145.9 82.9 %reduce-scatter.10.cloned.1.call-done = f32[144,512]{1,0:T(8,128)} async-done(((f32[2304,512]{1,0:T(8,128)}), f32[144,512]{1,0:T(8,128)}) %reduce-scatter.10.cloned.1.call-update) | async-done | bytes 294928 | tf_op jit(solution)/shard_map/reduce_scatter | solution.py:30
  228.8 0.0 all-gather.10.cloned.1.call-update
  228.9 0.2 all-reduce.6.cloned.1.call-start
  229.7 58.0 %all-gather.10.cloned.1.call-done = f32[2304,512]{1,0:T(8,128)} async-done(((f32[144,512]{1,0:T(8,128)}), f32[2304,512]{1,0:T(8,128)}) %all-gather.10.cloned.1.call-update) | async-done | bytes 4718608 | tf_op jit(solution)/shard_map/all_gather | solution.py:33
  287.8 6.9 multiply_reduce_fusion.5
  294.7 28.1 %all-gather.1 = f32[8192]{0:T(1024)S(1)} all-gather(f32[1024]{0:T(1024)S(1)} %pad_maximum_fusion), channel_id=3, replica_groups=mesh['row'=8,'col'=16] {'row'}, dimensions={0}, use_global_device_ids=true | all-gather | bytes 36864 | tf_op jit(solution)/shard_map/all_gather | solution.py:14
  322.8 6.9 multiply_subtract_fusion.1
  329.7 0.0 copy-start.1
  329.8 2.1 copy-done.1
  331.9 1.7 dynamic-slice_select_fusion.1
  333.5 0.0 all-reduce.6.cloned.1.call-update
  333.5 0.0 reduce-scatter.12.cloned.1.call-start
  333.6 82.1 %all-reduce.6.cloned.1.call-done = f32[1152,512]{1,0:T(8,128)} async-done(((f32[1152,512]{1,0:T(8,128)}), f32[1152,512]{1,0:T(8,128)}) %all-reduce.6.cloned.1.call-update) | async-done | bytes 2359312 | tf_op jit(solution)/shard_map/psum | solution.py:20
  415.7 37.5 %convolution_bitcast_fusion.1 = f32[2304,512]{0,1:T(8,128)} fusion(f32[1152,512]{1,0:T(8,128)} %all-reduce.6.cloned.1.call-done, f32[2304,1152]{1,0:T(8,128)} %param.4), kind=kOutput, calls=%fused_computation.1 | convolution fusion | flops 16307453952 | bytes 17694720 | tf_op jit(solution)/shard_map/dot_general | solution.py:57
  453.1 6.1 copy.16
  459.2 0.0 reduce-scatter.12.cloned.1.call-update
  459.2 0.0 all-gather.12.cloned.1.call-start
  459.3 83.0 %reduce-scatter.12.cloned.1.call-done = f32[144,512]{1,0:T(8,128)} async-done(((f32[2304,512]{1,0:T(8,128)}), f32[144,512]{1,0:T(8,128)}) %reduce-scatter.12.cloned.1.call-update) | async-done | bytes 294928 | tf_op jit(solution)/shard_map/reduce_scatter | solution.py:30
  542.2 0.0 all-gather.12.cloned.1.call-update
  542.3 0.3 all-reduce.8.cloned.1.call-start
  542.5 58.1 %all-gather.12.cloned.1.call-done = f32[2304,512]{1,0:T(8,128)} async-done(((f32[144,512]{1,0:T(8,128)}), f32[2304,512]{1,0:T(8,128)}) %all-gather.12.cloned.1.call-update) | async-done | bytes 4718608 | tf_op jit(solution)/shard_map/all_gather | solution.py:33
  600.6 6.9 multiply_reduce_fusion.3
  607.6 28.1 %all-gather.3 = f32[8192]{0:T(1024)S(1)} all-gather(f32[1024]{0:T(1024)S(1)} %pad_maximum_fusion.1), channel_id=5, replica_groups=mesh['row'=8,'col'=16] {'row'}, dimensions={0}, use_global_device_ids=true | all-gather | bytes 36864 | tf_op jit(solution)/shard_map/all_gather | solution.py:14
  635.7 8.7 multiply_subtract_fusion
  644.4 0.0 copy-start.2
  644.4 2.2 copy-done.2
  646.6 1.7 dynamic-slice_select_fusion
  648.2 0.0 all-reduce.8.cloned.1.call-update
  648.2 0.0 reduce-scatter.14.cloned.1.call-start
  648.3 82.1 %all-reduce.8.cloned.1.call-done = f32[1152,512]{1,0:T(8,128)} async-done(((f32[1152,512]{1,0:T(8,128)}), f32[1152,512]{1,0:T(8,128)}) %all-reduce.8.cloned.1.call-update) | async-done | bytes 2359312 | tf_op jit(solution)/shard_map/psum | solution.py:20
  730.4 37.5 %convolution_bitcast_fusion = f32[2304,512]{0,1:T(8,128)} fusion(f32[1152,512]{1,0:T(8,128)} %all-reduce.8.cloned.1.call-done, f32[2304,1152]{1,0:T(8,128)} %param.4), kind=kOutput, calls=%fused_computation | convolution fusion | flops 16307453952 | bytes 17694720 | tf_op jit(solution)/shard_map/dot_general | solution.py:57
  767.8 6.1 copy.18
  773.9 0.0 reduce-scatter.14.cloned.1.call-update
  773.9 0.3 all-gather.14.cloned.1.call-start
  774.2 82.7 %reduce-scatter.14.cloned.1.call-done = f32[144,512]{1,0:T(8,128)} async-done(((f32[2304,512]{1,0:T(8,128)}), f32[144,512]{1,0:T(8,128)}) %reduce-scatter.14.cloned.1.call-update) | async-done | bytes 294928 | tf_op jit(solution)/shard_map/reduce_scatter | solution.py:30
  856.9 0.0 all-gather.14.cloned.1.call-update
  856.9 58.9 %all-gather.14.cloned.1.call-done = f32[2304,512]{1,0:T(8,128)} async-done(((f32[144,512]{1,0:T(8,128)}), f32[2304,512]{1,0:T(8,128)}) %all-gather.14.cloned.1.call-update) | async-done | bytes 4718608 | tf_op jit(solution)/shard_map/all_gather | solution.py:33
  915.8 6.9 multiply_reduce_fusion.1
  922.8 28.1 %all-gather.5 = f32[8192]{0:T(1024)S(1)} all-gather(f32[1024]{0:T(1024)S(1)} %pad_maximum_fusion.2), channel_id=7, replica_groups=mesh['row'=8,'col'=16] {'row'}, dimensions={0}, use_global_device_ids=true | all-gather | bytes 36864 | tf_op jit(solution)/shard_map/all_gather | solution.py:14
  950.9 9.2 multiply_add_fusion
  (12 shorter events, 0.2 us)
Async XLA Ops:
  6.5 95.7 %all-reduce.4.cloned.1.call-start = ((), (), s32[]{:S(2)}) async-start(), calls=%async_computation.3 | async-start | bytes 4718592 | tf_op jit(solution)/shard_map/psum | solution.py:20
  11.5 2.2 copy-start
  15.4 213.5 %reduce-scatter.10.cloned.1.call-start = ((), (), s32[]{:S(2)}) async-start(), calls=%async_computation.9 | async-start | bytes 5013504 | tf_op jit(solution)/shard_map/reduce_scatter | solution.py:30
  145.9 141.9 %all-gather.10.cloned.1.call-start = ((), (), s32[]{:S(2)}) async-start(), calls=%async_computation.6 | async-start | bytes 5013504 | tf_op jit(solution)/shard_map/all_gather | solution.py:33
  228.9 186.8 %all-reduce.6.cloned.1.call-start = ((), (), s32[]{:S(2)}) async-start(), calls=%async_computation.4 | async-start | bytes 4718592 | tf_op jit(solution)/shard_map/psum | solution.py:20
  329.7 2.1 copy-start.1
  333.5 208.7 %reduce-scatter.12.cloned.1.call-start = ((), (), s32[]{:S(2)}) async-start(), calls=%async_computation.10 | async-start | bytes 5013504 | tf_op jit(solution)/shard_map/reduce_scatter | solution.py:30
  459.2 141.4 %all-gather.12.cloned.1.call-start = ((), (), s32[]{:S(2)}) async-start(), calls=%async_computation.7 | async-start | bytes 5013504 | tf_op jit(solution)/shard_map/all_gather | solution.py:33
  542.3 188.1 %all-reduce.8.cloned.1.call-start = ((), (), s32[]{:S(2)}) async-start(), calls=%async_computation.5 | async-start | bytes 4718592 | tf_op jit(solution)/shard_map/psum | solution.py:20
  644.4 2.2 copy-start.2
  648.2 208.7 %reduce-scatter.14.cloned.1.call-start = ((), (), s32[]{:S(2)}) async-start(), calls=%async_computation.11 | async-start | bytes 5013504 | tf_op jit(solution)/shard_map/reduce_scatter | solution.py:30
  773.9 141.9 %all-gather.14.cloned.1.call-start = ((), (), s32[]{:S(2)}) async-start(), calls=%async_computation.8 | async-start | bytes 5013504 | tf_op jit(solution)/shard_map/all_gather | solution.py:33
Sparse Core Ops, SparseCore 0:
  15.5 86.6 all-reduce.3
  146.0 82.7 reduce-scatter.9
  231.6 56.1 all-gather.9
  333.7 81.9 all-reduce.5
  459.4 82.8 reduce-scatter.11
  544.6 56.0 all-gather.11
  648.4 81.9 all-reduce.7
  774.1 82.8 reduce-scatter.13
  859.7 56.0 all-gather.13
